TPU v7x, 512 devices: a whole 4x4x16 slice. The times are simulated.
512 devices in a mesh: tp: 8 (over x, core), ep: 64 (over z, y).
Axes of the slice: x: 4, y: 4, z: 16, core: 2. Of those that a mesh axis runs over, the one named last changes fastest.
Arguments:
- hidden_in: bfloat16 [4096, 4096], P(('ep', 'tp')), may hold values from -6 to 6
- norm_gain: bfloat16 [4096], replicated, may hold values from 0.099609375 to 1.8984375
- expert_ids: int32 [4096, 8], P('ep'), may hold values from 0 to 63, all different within a row; in each aligned block of 64 rows (0 to 63, 64 to 127, ...) at most 16 rows name the same one
- gate_weights: float32 [4096, 8], P('ep'), may hold values from 0.05 to 0.35
- w_gate: bfloat16 [64, 4096, 1024], P('ep', None, 'tp'), may hold values from -0.09375 to 0.09375
- w_up: bfloat16 [64, 4096, 1024], P('ep', None, 'tp'), may hold values from -0.09375 to 0.09375
- w_down: bfloat16 [64, 1024, 4096], P('ep', None, 'tp'), may hold values from -0.1875 to 0.1875
Outputs:
- mixed: bfloat16 [4096, 4096], P('ep', 'tp')
Inputs may be any that keep to these rules, and one draw needn't show every extreme that they name: `expert_ids`: each row names 8 different experts. Tokens form groups of 64 consecutive rows; within one group no expert is named by more than 16 rows, and in every draw some expert is named by exactly 16 rows of some group.
All inputs are finite; a program needn't handle non-finite values.
Results may differ from a plain program's by a relative error of at most 0.0043.
Values may be sent and summed in bfloat16 or wider, within the bound.
A program may use at most 64 MiB of HBM per device.

v0:
```python
import jax
import jax.numpy as jnp
from jax import lax
from jax.sharding import PartitionSpec as P


def shards(hidden_in, norm_gain, expert_ids, gate_weights, w_gate, w_up, w_down):
    n_ep = lax.axis_size("ep")
    tp_pos = lax.axis_index("tp")
    tok_dev, width = hidden_in.shape
    group, top = expert_ids.shape
    exp_loc, _, hid_part = w_gate.shape
    col_part = w_down.shape[2]
    experts = exp_loc * n_ep
    cap = max(2, 2 * top * group // experts)
    values = hidden_in.astype(jnp.float32)
    scale = lax.rsqrt(jnp.mean(values * values, axis=1, keepdims=True) + 1e-06)
    normed = (values * scale * norm_gain.astype(jnp.float32)).astype(jnp.bfloat16)
    flat_ids = expert_ids.reshape(-1)
    pairs = flat_ids.shape[0]
    hits = (flat_ids[:, None] == lax.broadcasted_iota(jnp.int32, (pairs, experts), 1)).astype(
        jnp.int32
    )
    before = jnp.cumsum(hits, axis=0) - hits
    position = jnp.sum(before * hits, axis=1)
    slot_index = flat_ids * cap + position
    places = lax.broadcasted_iota(jnp.int32, (experts * cap, group, top), 0)
    dispatch_map = jnp.any(places == slot_index.reshape(group, top)[None], axis=2).astype(
        jnp.bfloat16
    )
    whole_norm, whole_input = (
        lax.all_gather(normed, "tp", axis=0, tiled=True),
        lax.all_gather(hidden_in, "tp", axis=0, tiled=True),
    )
    residual = lax.dynamic_slice_in_dim(whole_input, tp_pos * col_part, col_part, 1)
    packed = jnp.dot(dispatch_map, whole_norm, preferred_element_type=jnp.float32).astype(
        jnp.bfloat16
    )
    packed = packed.reshape(n_ep, exp_loc, cap, width)
    arrived = lax.all_to_all(packed, "ep", split_axis=0, concat_axis=0, tiled=True)
    gate_act = jnp.einsum("secd,edh->sech", arrived, w_gate, preferred_element_type=jnp.float32)
    up_act = jnp.einsum("secd,edh->sech", arrived, w_up, preferred_element_type=jnp.float32)
    hidden = (jax.nn.silu(gate_act) * up_act).astype(jnp.bfloat16)
    outputs = jnp.einsum(
        "sech,ehf->secf",
        lax.all_gather(hidden, "tp", axis=3, tiled=True),
        w_down,
        preferred_element_type=jnp.float32,
    )
    returned = lax.all_to_all(
        outputs.astype(jnp.bfloat16), "ep", split_axis=0, concat_axis=0, tiled=True
    )
    flat_back = returned.reshape(experts * cap, col_part)
    picked = flat_back[slot_index].reshape(group, top, col_part).astype(jnp.float32)
    combined = jnp.sum(picked * gate_weights[:, :, None], axis=1)
    return (residual.astype(jnp.float32) + combined).astype(jnp.bfloat16)


def solution(mesh):
    in_specs = (
        P(("ep", "tp"), None),
        P(),
        P("ep", None),
        P("ep", None),
        P("ep", None, "tp"),
        P("ep", None, "tp"),
        P("ep", None, "tp"),
    )
    out_specs = P("ep", "tp")
    return jax.shard_map(shards, mesh=mesh, in_specs=in_specs, out_specs=out_specs, check_vma=False)
```

profile of v0, /device:TPU:8, one launch (start us, length us, event | category | flops | bytes accessed | tf_op | source)
XLA Modules:
  0.0 533.4 jit_solution(16450931015749666999)
XLA Ops:
  6.5 0.0 copy-start
  6.5 0.0 all-gather.2.cloned.1.call-start
  6.5 0.9 copy.22
  7.4 0.1 eq.29
  7.5 0.1 eq.26
  7.6 1.2 reduce-window.6
  8.8 0.2 slice_reduce_fusion
  9.1 0.1 fusion.34
  9.2 0.1 reduce_sum.32
  9.3 0.7 fusion.6
  10.0 0.7 convert_element_type.51
  10.7 1.0 fusion.29
  11.7 0.9 fusion.31
  12.6 13.5 %all_gather.10 = bf16[64,4096]{1,0:T(8,128)(2,1)S(1)} all-gather(bf16[8,4096]{1,0:T(8,128)(2,1)S(1)} %fusion.31), channel_id=1, replica_groups=mesh['tp'=8,'ep'=64] {'tp'}, dimensions={0}, use_global_device_ids=true | all-gather | bytes 589824 | tf_op jit(solution)/shard_map/all_gather | solution.py:32
  26.1 2.4 convolution_convert_fusion
  28.5 0.0 copy-start.3
  28.5 388.9 %all_to_all.10 = bf16[64,1,16,4096]{3,2,1,0:T(8,128)(2,1)S(1)} all-to-all(bf16[64,1,16,4096]{3,2,1,0:T(8,128)(2,1)S(1)} %bitcast.86), channel_id=1, replica_groups=mesh['tp'=8,'ep'=64] {'ep'}, dimensions={0} | all-to-all | bytes 16777216 | tf_op jit(solution)/shard_map/all_to_all | solution.py:40
  417.4 0.0 copy-done.3
  417.4 0.0 copy-start.4
  417.4 2.3 fusion.13
  419.8 0.0 copy-done.4
  419.8 3.1 fusion.22
  422.9 0.0 copy-start.2
  422.9 0.0 copy-start.1
  422.9 0.0 all-gather.2.cloned.1.call-update
  422.9 25.6 %all-gather.2.cloned.1.call-done = bf16[64,1,16,1024]{3,2,0,1:T(8,128)(2,1)} async-done(((bf16[64,1,16,128]{3,2,0,1:T(8,128)(2,1)}), bf16[64,1,16,1024]{3,2,0,1:T(8,128)(2,1)}) %all-gather.2.cloned.1.call-update) | async-done | bytes 2097168 | tf_op jit(solution)/shard_map/all_gather | solution.py:46
  448.5 0.0 copy-done
  448.5 3.8 fusion.10
  452.3 15.7 %all-to-all-start.1 = ((bf16[64,1,16,512]{3,2,1,0:T(8,128)(2,1)}), bf16[64,1,16,512]{3,2,1,0:T(8,128)(2,1)S(1)}, u32[]{:S(2)}, u32[]{:S(2)}) async-start(bf16[64,1,16,512]{3,2,1,0:T(8,128)(2,1)} %fusion.10), calls=%async_computation.1 | async-start | bytes 2097152 | tf_op jit(solution)/shard_map/all_to_all | solution.py:50
  468.0 0.1 mul.69
  468.1 0.0 copy-done.2
  468.1 0.1 copy.28
  468.2 0.0 copy-done.1
  468.2 13.1 %all_gather.9 = bf16[64,4096]{1,0:T(8,128)(2,1)S(1)} all-gather(bf16[8,4096]{1,0:T(8,128)(2,1)S(1)} %copy-done.1), channel_id=1, replica_groups=mesh['tp'=8,'ep'=64] {'tp'}, dimensions={0}, use_global_device_ids=true | all-gather | bytes 589824 | tf_op jit(solution)/shard_map/all_gather | solution.py:33
  481.3 42.2 %all-to-all-done.1 = bf16[64,1,16,512]{3,2,1,0:T(8,128)(2,1)S(1)} async-done(((bf16[64,1,16,512]{3,2,1,0:T(8,128)(2,1)}), bf16[64,1,16,512]{3,2,1,0:T(8,128)(2,1)S(1)}, u32[]{:S(2)}, u32[]{:S(2)}) %all-to-all-start.1) | async-done | bytes 1048608 | tf_op jit(solution)/shard_map/all_to_all | solution.py:50
  523.6 2.0 gather_fusion
  525.6 0.4 fusion.25
  525.9 0.7 add_convert_fusion
  (7 shorter events, 0.1 us)
Async XLA Ops:
  6.5 441.9 %copy-start = (bf16[1,1024,512]{2,1,0:T(8,128)(2,1)S(1)}, bf16[1,1024,512]{2,1,0:T(8,128)(2,1)}, u32[]{:S(2)}) copy-start(bf16[1,1024,512]{2,1,0:T(8,128)(2,1)} %param.13) | copy-start | bytes 3145732
  6.5 441.9 %all-gather.2.cloned.1.call-start = ((), (), s32[]{:S(2)}) async-start(), calls=%async_computation.2 | async-start | bytes 2359296 | tf_op jit(solution)/shard_map/all_gather | solution.py:46
  28.5 388.9 %copy-start.3 = (bf16[1,4096,128]{2,1,0:T(8,128)(2,1)S(1)}, bf16[1,4096,128]{2,1,0:T(8,128)(2,1)}, u32[]{:S(2)}) copy-start(bf16[1,4096,128]{2,1,0:T(8,128)(2,1)} %param.11) | copy-start | bytes 3145732
  417.4 2.3 copy-start.4
  422.9 45.3 %copy-start.2 = (f32[64,8]{0,1:T(8,128)S(1)}, f32[64,8]{0,1:T(8,128)}, u32[]{:S(2)}) copy-start(f32[64,8]{0,1:T(8,128)} %param.10) | copy-start | bytes 6148
  422.9 45.4 %copy-start.1 = (bf16[8,4096]{1,0:T(8,128)(2,1)S(1)}, bf16[8,4096]{1,0:T(8,128)(2,1)}, u32[]{:S(2)}) copy-start(bf16[8,4096]{1,0:T(8,128)(2,1)} %param.7) | copy-start | bytes 196612
  452.3 71.3 %all-to-all-start.1 = ((bf16[64,1,16,512]{3,2,1,0:T(8,128)(2,1)}), bf16[64,1,16,512]{3,2,1,0:T(8,128)(2,1)S(1)}, u32[]{:S(2)}, u32[]{:S(2)}) async-start(bf16[64,1,16,512]{3,2,1,0:T(8,128)(2,1)} %fusion.10), calls=%async_computation.1 | async-start | bytes 2097152 | tf_op jit(solution)/shard_map/all_to_all | solution.py:50
Sparse Core Ops, SparseCore 0:
  423.0 25.4 all-gather.1
where the time goes:
time: 534 us; the launch traced here: 533 us
  blocking collectives  416 us (78%)
  waiting for transfers between devices  67.8 us (13%)
  starting transfers between devices  15.7 us (3%)
  between operations  13.5 us (3%)
  matrix products  11.6 us (2%)
  other arithmetic  5.74 us (1%)
    all_to_all x1, blocking collectives, shards(): lax.all_to_all(packed, 'ep', split_axis=0, concat_axis=0, tiled=True)  389 us
    all_to_all x1, waiting for transfers between devices, shards(): lax.all_to_all(outputs.astype(jnp.bfloat16), 'ep', split_axis=0, concat_a...  42.2 us
    all_gather x1, waiting for transfers between devices, shards(): lax.all_gather(hidden, 'tp', axis=3, tiled=True)  25.6 us
    all_to_all x1, starting transfers between devices, shards(): lax.all_to_all(outputs.astype(jnp.bfloat16), 'ep', split_axis=0, concat_a...  15.7 us
    all_gather x1, blocking collectives, shards(): lax.all_gather(normed, 'tp', axis=0, tiled=True)  13.5 us
    all_gather x1, blocking collectives, shards(): lax.all_gather(hidden_in, 'tp', axis=0, tiled=True)  13.1 us
  transfers between devices with their start and end apart: 2, of which 2 were waited for; matrix products, arithmetic and copies ran while one was open for 0% of the time, Pallas kernels for 0%

commit v1 on v0

v1 whole, which is shorter than its diff:
```python
import functools

import jax
import jax.numpy as jnp
from jax import lax
from jax.experimental import pallas as pl
from jax.experimental.pallas import tpu as pltpu
from jax.sharding import PartitionSpec as P

MESH = pl.DeviceIdType.MESH
F32, BF16 = jnp.float32, jnp.bfloat16
STEPS = 8
AT = dict(Y=1, X1=3, X2=5, M=6, H2=8, D=9, C=11)


def kernel(
    hid_ref, gain_ref, ids_ref, gat_ref, wg_ref, wu_ref, wd_ref, out_ref,
    hq, scl, ring_a, ring_b, meta_a, meta_b, pick, ybuf, xfull, hfull, obuf, oin, cbuf, own, zin_a, zin_b,
    wcat, wdv, tri,
    wsem, p_s, p_r, za_s, za_r, zb_s, zb_r, y_s, y_r, x_s, x_r, h_s, h_r, o_s, o_r, ra_s, ra_r, rb_s, rb_r,
):
    tp, ep = lax.axis_index("tp"), lax.axis_index("ep")
    x, c = tp // 2, lax.rem(tp, 2)
    z, y = ep // 4, lax.rem(ep, 4)
    quarter = lax.rem(tp, 4)
    across = lax.rem(quarter + 2, 4)

    def at_tp(r):
        return (lax.rem(tp + r + 8, 8), ep)

    def at_x(r):
        return (lax.rem(x + r + 4, 4) * 2 + c, ep)

    def at_y(r):
        return (tp, z * 4 + lax.rem(y + r, 4))

    def at_z(r):
        return (tp, lax.rem(z + r + 16, 16) * 4 + y)

    partner = (x * 2 + 1 - c, ep)

    def move(src, dst, send, recv, device):
        return pltpu.make_async_remote_copy(
            src_ref=src, dst_ref=dst, send_sem=send, recv_sem=recv, device_id=device, device_id_type=MESH
        )

    barrier = pltpu.get_barrier_semaphore()
    peers = [at_tp(r) for r in range(1, 8)] + [at_y(r) for r in range(1, 4)]
    peers += [at_z(r) for r in (-4, -3, -2, -1, 1, 2, 3, 4)]
    for peer in peers:
        pl.semaphore_signal(barrier, inc=1, device_id=peer, device_id_type=MESH)

    loads = []
    for q in range(4):
        for b in range(2):
            rows = pl.ds((q + 4 * b) * 512, 512)
            for n, w in enumerate((wg_ref, wu_ref)):
                loads.append(
                    pltpu.make_async_copy(
                        w.at[0, rows, :], wcat.at[q, pl.ds(b * 512, 512), pl.ds(n * 128, 128)], wsem.at[len(loads)]
                    )
                )
    loads.append(pltpu.make_async_copy(wd_ref.at[0], wdv, wsem.at[16]))
    for load in loads:
        load.start()

    values = hid_ref[...].astype(F32)
    scale = lax.rsqrt(jnp.mean(values * values, axis=1, keepdims=True) + 1e-06)
    scl[tp] = jnp.broadcast_to(scale, (8, 128))
    for b in range(2):
        hq[tp, b] = hid_ref[:, pl.ds(pl.multiple_of((quarter + 4 * b) * 512, 512), 512)]
    ids, gates = ids_ref[...].astype(F32), gat_ref[...]
    meta = jnp.concatenate(
        [jnp.concatenate([ids, ids], axis=1), jnp.concatenate([gates, gates], axis=1)], axis=0
    )
    meta_a[0] = meta
    meta_b[0] = meta
    before, after = lax.broadcasted_iota(jnp.int32, (128, 128), 0), lax.broadcasted_iota(jnp.int32, (128, 128), 1)
    tri[...] = ((before < after) & ((before < 64) == (after < 64))).astype(F32).astype(BF16)
    pl.semaphore_wait(barrier, len(peers))

    def spread(r, b):
        device = at_tp(r)
        if b == 2:
            src, dst = scl.at[tp], scl.at[tp]
        else:
            block = lax.rem(device[0], 4) + 4 * b
            src, dst = hid_ref.at[:, pl.ds(pl.multiple_of(block * 512, 512), 512)], hq.at[tp, b]
        return move(src, dst, p_s.at[r - 1, b], p_r.at[r - 1, b], device)

    for r in range(1, 8):
        for b in range(3):
            spread(r, b).start()
    for r in range(1, 8):
        for b in range(3):
            spread(r, b).wait_recv()
    scales = scl[...]
    scales = jnp.concatenate([scales] * 4, axis=2)
    for b in range(2):
        gain = gain_ref[pl.ds(quarter + 4 * b, 1), :]
        normed = (hq[:, b].astype(F32) * scales).reshape(64, 512) * gain
        normed = normed.astype(BF16)
        ring_a[0, b] = normed
        ring_b[0, b] = normed
    for load in loads:
        load.wait()

    def up(i, b):
        if b == 2:
            src, dst = meta_a.at[i], meta_a.at[i + 1]
        else:
            src, dst = ring_a.at[i, b], ring_a.at[i + 1, b]
        return move(src, dst, za_s.at[i, b], za_r.at[i, b], at_z(1))

    def down(i, b):
        if b == 2:
            src, dst = meta_b.at[i], meta_b.at[i + 1]
        else:
            src, dst = ring_b.at[i, b], ring_b.at[i + 1, b]
        return move(src, dst, zb_s.at[i, b], zb_r.at[i, b], at_z(-1))

    def to_y(j, r):
        device = at_y(r)
        there = lax.rem(y + r, 4)
        dst = xfull.at[j, quarter, pl.ds(pl.multiple_of(y * 32, 32), 32), :]
        return move(ybuf.at[j, there], dst, y_s.at[j, r - 1], y_r.at[j, r - 1], device)

    def to_x(j, n):
        if n == 0:
            part, device = xfull.at[j, quarter, pl.ds(0, 64), :], at_x(1)
        elif n == 1:
            part, device = xfull.at[j, quarter, pl.ds(64, 64), :], at_x(-1)
        elif n == 2:
            part, device = xfull.at[j, quarter], partner
        else:
            part, device = xfull.at[j, across], partner
        return move(part, part, x_s.at[j, n], x_r.at[j, n], device)

    def to_h(j, n):
        if n < 3:
            part, device = hfull.at[j, tp], at_x(n + 1)
        elif n == 3:
            part, device = hfull.at[j, tp], partner
        else:
            part, device = hfull.at[j, lax.rem(tp - 2 * (n - 3) + 8, 8)], partner
        return move(part, part, h_s.at[j, n], h_r.at[j, n], device)

    def to_o(j, r):
        return move(obuf.at[j, lax.rem(y + r, 4)], oin.at[j, y], o_s.at[j, r - 1], o_r.at[j, r - 1], at_y(r))

    def home_a(j, hops):
        return move(cbuf.at[j, 0], zin_a.at[j], ra_s.at[j], ra_r.at[j], at_z(-hops))

    def home_b(j, hops):
        return move(cbuf.at[j, 1], zin_b.at[j], rb_s.at[j], rb_r.at[j], at_z(hops))

    def stage_y(j):
        first = lax.broadcasted_iota(jnp.int32, (8, 128), 1) < 64
        ids = jnp.where(first, meta_a[j + 1, 0:8, :], meta_b[j, 0:8, :])
        gates = jnp.where(first, meta_a[j + 1, 8:16, :], meta_b[j, 8:16, :])
        row = lax.broadcasted_iota(jnp.int32, (16, 128), 0)
        hits, weights, table = [], [], jnp.zeros((16, 128), F32)
        for n in range(4):
            same = ids == (z * 4 + n).astype(F32)
            hits.append(jnp.sum(jnp.where(same, 1.0, 0.0), axis=0, keepdims=True))
            weights.append(jnp.sum(jnp.where(same, gates, 0.0), axis=0, keepdims=True))
            table = jnp.where(row == n, hits[n], table)
        places = jnp.dot(table.astype(BF16), tri[...], preferred_element_type=F32)
        slot = lax.broadcasted_iota(jnp.int32, (32, 128), 0).astype(F32)
        shift = jnp.where(first[0:1], 0.0, 16.0)
        chosen, weighted = [], []
        for n in range(4):
            mine = jnp.where(hits[n] > 0.5, places[n : n + 1] + shift, -1.0)
            chosen.append(jnp.where(slot == mine, 1.0, 0.0))
            weighted.append(chosen[n] * weights[n])
        chosen = jnp.concatenate(chosen, axis=0).astype(BF16)
        weighted = jnp.concatenate(weighted, axis=0)
        high = weighted.astype(BF16)
        pick[j, 0] = high
        pick[j, 1] = (weighted - high.astype(F32)).astype(BF16)
        for b in range(2):
            tokens = jnp.concatenate([ring_a[j + 1, b], ring_b[j, b]], axis=0)
            rows = jnp.dot(chosen, tokens, preferred_element_type=F32).astype(BF16)
            ybuf[j, :, :, pl.ds(b * 512, 512)] = rows.reshape(4, 32, 512)
        xfull[j, quarter, pl.ds(pl.multiple_of(y * 32, 32), 32), :] = ybuf[j, y]
        for r in range(1, 4):
            to_y(j, r).start()

    def stage_x1(j):
        for r in range(1, 4):
            to_y(j, r).wait_recv()
        for n in range(3):
            to_x(j, n).start()

    def stage_x2(j):
        for n in range(2):
            wait_x(j, n)
        to_x(j, 3).start()

    def wait_x(j, n):
        part = xfull.at[j, across, pl.ds(64 * n, 64), :]
        move(part, part, x_s.at[j, n], x_r.at[j, n], partner).wait_recv()

    def stage_m(j):
        for n in range(2, 4):
            to_x(j, n).wait_recv()
        total = jnp.zeros((128, 256), F32)
        for q in range(4):
            total += jnp.dot(xfull[j, q], wcat[q], preferred_element_type=F32)
        gate, lift = total[:, :128], total[:, 128:]
        hfull[j, tp] = (gate / (1.0 + jnp.exp(-gate)) * lift).astype(BF16)
        for n in range(4):
            to_h(j, n).start()

    def stage_h2(j):
        for n in range(3):
            to_h(j, n).wait_recv()
        for n in range(4, 7):
            to_h(j, n).start()

    def stage_d(j):
        for n in range(3, 7):
            to_h(j, n).wait_recv()
        units = jnp.concatenate([hfull[j, n] for n in range(8)], axis=1)
        rows = jnp.dot(units, wdv[...], preferred_element_type=F32).astype(BF16)
        obuf[j] = rows.reshape(4, 32, 512)
        oin[j, y] = obuf[j, y]
        for r in range(1, 4):
            to_o(j, r).start()

    def stage_c(j):
        for r in range(1, 4):
            to_o(j, r).wait_recv()
        rows = oin[j].reshape(128, 512)
        dims = (((0,), (0,)), ((), ()))
        total = lax.dot_general(pick[j, 0], rows, dims, preferred_element_type=F32)
        total += lax.dot_general(pick[j, 1], rows, dims, preferred_element_type=F32)
        cbuf[j, 0] = total[:64].astype(BF16)
        cbuf[j, 1] = total[64:].astype(BF16)

        @pl.when(j < 3)
        def _():
            home_a(j, j + 1).start()

        @pl.when(j == 3)
        def _():
            own[0] = total[:64]

        @pl.when(j > 3)
        def _():
            home_a(j, j - 3).start()

        @pl.when(j == 0)
        def _():
            own[1] = total[64:]

        @pl.when((j > 0) & (j < 4))
        def _():
            home_b(j, j).start()

        @pl.when(j == 4)
        def _():
            own[2] = total[64:]

        @pl.when(j > 4)
        def _():
            home_b(j, j - 4).start()

    def stage(name, body, i):
        j = i - AT[name]

        @pl.when((j >= 0) & (j < STEPS))
        def _():
            body(j)

    @pl.loop(0, STEPS + AT["C"])
    def _(i):
        @pl.when(i <= STEPS)
        def _():
            for b in (2, 0, 1):

                @pl.when(i > 0)
                def _():
                    up(i - 1, b).wait_recv()

                @pl.when(i < STEPS)
                def _():
                    up(i, b).start()

                @pl.when((i > 0) & (i < STEPS))
                def _():
                    down(i - 1, b).wait_recv()

                @pl.when(i < STEPS - 1)
                def _():
                    down(i, b).start()

        stage("Y", stage_y, i)
        stage("X1", stage_x1, i)
        stage("X2", stage_x2, i)
        stage("H2", stage_h2, i)
        stage("D", stage_d, i)
        stage("M", stage_m, i)
        stage("C", stage_c, i)

    total = own[0]
    for j in range(4, 8):
        home_a(j, 0).wait_recv()
        total += zin_a[j].astype(F32)
    cbuf[3, 0] = total.astype(BF16)
    home_a(3, 4).start()
    total = own[2]
    for j in range(5, 8):
        home_b(j, 0).wait_recv()
        total += zin_b[j].astype(F32)
    cbuf[4, 1] = total.astype(BF16)
    home_b(4, 4).start()

    total = own[1] + hq[:, tp // 4].astype(F32).reshape(64, 512)
    for j in range(3):
        home_a(j, 0).wait_recv()
        total += zin_a[j].astype(F32)
    for j in range(1, 4):
        home_b(j, 0).wait_recv()
        total += zin_b[j].astype(F32)
    home_a(3, 4).wait_recv()
    home_b(4, 4).wait_recv()
    out_ref[...] = (total + zin_a[3].astype(F32) + zin_b[4].astype(F32)).astype(BF16)

    for r in range(1, 8):
        for b in range(3):
            spread(r, b).wait_send()

    @pl.loop(0, STEPS)
    def _(j):
        for b in range(3):
            up(j, b).wait_send()

            @pl.when(j < STEPS - 1)
            def _():
                down(j, b).wait_send()

        for r in range(1, 4):
            to_y(j, r).wait_send()
            to_o(j, r).wait_send()
        for n in range(4):
            to_x(j, n).wait_send()
        for n in range(7):
            to_h(j, n).wait_send()
        home_a(j, 1).wait_send()

        @pl.when(j > 0)
        def _():
            home_b(j, 1).wait_send()


def shards(hidden_in, norm_gain, expert_ids, gate_weights, w_gate, w_up, w_down):
    vmem, hbm = pl.BlockSpec(memory_space=pltpu.VMEM), pl.BlockSpec(memory_space=pl.ANY)
    dma = pltpu.SemaphoreType.DMA
    return pl.pallas_call(
        kernel,
        out_shape=jax.ShapeDtypeStruct((64, 512), BF16),
        in_specs=[vmem] * 4 + [hbm] * 3,
        out_specs=vmem,
        scratch_shapes=[
            pltpu.VMEM((8, 2, 8, 512), BF16),
            pltpu.VMEM((8, 8, 128), F32),
            pltpu.VMEM((9, 2, 64, 512), BF16),
            pltpu.VMEM((8, 2, 64, 512), BF16),
            pltpu.VMEM((9, 16, 128), F32),
            pltpu.VMEM((8, 16, 128), F32),
            pltpu.VMEM((8, 2, 128, 128), BF16),
            pltpu.VMEM((8, 4, 32, 1024), BF16),
            pltpu.VMEM((8, 4, 128, 1024), BF16),
            pltpu.VMEM((8, 8, 128, 128), BF16),
            pltpu.VMEM((8, 4, 32, 512), BF16),
            pltpu.VMEM((8, 4, 32, 512), BF16),
            pltpu.VMEM((8, 2, 64, 512), BF16),
            pltpu.VMEM((3, 64, 512), F32),
            pltpu.VMEM((8, 64, 512), BF16),
            pltpu.VMEM((8, 64, 512), BF16),
            pltpu.VMEM((4, 1024, 256), BF16),
            pltpu.VMEM((1024, 512), BF16),
            pltpu.VMEM((128, 128), BF16),
            dma((17,)),
            dma((7, 3)), dma((7, 3)),
            dma((8, 3)), dma((8, 3)),
            dma((7, 3)), dma((7, 3)),
            dma((8, 3)), dma((8, 3)),
            dma((8, 4)), dma((8, 4)),
            dma((8, 7)), dma((8, 7)),
            dma((8, 3)), dma((8, 3)),
            dma((8,)), dma((8,)),
            dma((8,)), dma((8,)),
        ],
        compiler_params=pltpu.CompilerParams(
            collective_id=0, has_side_effects=True, vmem_limit_bytes=56 * 1024 * 1024
        ),
    )(
        hidden_in,
        norm_gain.astype(F32).reshape(8, 512),
        expert_ids.T,
        gate_weights.T,
        w_gate,
        w_up,
        w_down,
    )


def solution(mesh):
    in_specs = (
        P(("ep", "tp"), None),
        P(),
        P("ep", None),
        P("ep", None),
        P("ep", None, "tp"),
        P("ep", None, "tp"),
        P("ep", None, "tp"),
    )
    return jax.shard_map(shards, mesh=mesh, in_specs=in_specs, out_specs=P("ep", "tp"), check_vma=False)
```

time: 534 us -> 109 us (0.20)
  the two profiles are of different devices: /device:TPU:8 before, /device:TPU:1 now
where the time goes in v1:
time: 109 us
  Pallas kernels  106 us (97%)
  local copies, waits for them, and re-layouts  2.79 us (3%)
    pallas_call x1, Pallas kernels, shards(): pl.pallas_call(kernel, out_shape=jax.ShapeDtypeStruct((64, 512), BF16), i...  106 us

profile of v1, /device:TPU:1, one launch (start us, length us, event | category | flops | bytes accessed | tf_op | source)
XLA Modules:
  0.0 108.6 jit_solution(13321373482471725369)
XLA Ops:
  0.0 1.3 %reshape.8.gain_ref = f32[8,512]{1,0:T(8,128)} reshape(bf16[4096]{0:T(1024)(128)(2,1)} %param.8) | data formatting | bytes 24576 | tf_op jit(solution)/shard_map/reshape | solution.py:401
  1.3 105.8 %shard_map.73 = bf16[64,512]{1,0:T(8,128)(2,1)} custom-call(bf16[8,4096]{1,0:T(8,128)(2,1)} %hid_ref.1, f32[8,512]{1,0:T(8,128)} %reshape.8.gain_ref, s32[8,64]{1,0:T(8,128)} %bitcast.2, f32[8,64]{1,0:T(8,128)} %bitcast.3, bf16[1,4096,128]{2,1,0:T(8,128)(2,1)} %wg_ref.1, bf16[1,4096,128]{2,1,0:T(8,128)(2,1)} %wu_ref.1, bf16[1,1024,512]{2,1,0:T(8,128)(2,1)} %wd_ref.1), custom_call_target="tpu_custom_call" | custom-call | tf_op jit(solution)/shard_map/pallas_call | solution.py:360
  107.1 1.5 %copy.9 = bf16[64,512]{1,0:T(8,128)(2,1)} copy(bf16[64,512]{1,0:T(8,128)(2,1)} %shard_map.73) | data formatting | bytes 131072

commit v2 on v1

--- a/solution.py
+++ b/solution.py
@@ -10,7 +10,10 @@
 MESH = pl.DeviceIdType.MESH
 F32, BF16 = jnp.float32, jnp.bfloat16
 STEPS = 8
-AT = dict(Y=1, X1=3, X2=5, M=6, H2=8, D=9, C=11)
+PARTS = 4
+NEXT = {8: 6, 7: 6, 6: 3, 5: 3, 4: 3, 3: 0, 2: 0, 1: 0}
+HOLDS = sorted({d for d in NEXT.values() if d}, reverse=True)
+AT = dict(Y=1, X1=2, X2=4, M=5, H2=7, D=8, C=10)
 
 
 def kernel(
@@ -46,10 +49,30 @@
 
     barrier = pltpu.get_barrier_semaphore()
     peers = [at_tp(r) for r in range(1, 8)] + [at_y(r) for r in range(1, 4)]
-    peers += [at_z(r) for r in (-4, -3, -2, -1, 1, 2, 3, 4)]
+    hops = sorted({d - e for d, e in NEXT.items()} | {1})
+    peers += [at_z(r) for h in hops for r in (h, -h)]
     for peer in peers:
         pl.semaphore_signal(barrier, inc=1, device_id=peer, device_id_type=MESH)
 
+    values = hid_ref[...].astype(F32)
+    scale = lax.rsqrt(jnp.mean(values * values, axis=1, keepdims=True) + 1e-06)
+    scl[tp] = jnp.broadcast_to(scale, (8, 128))
+    for b in range(2):
+        hq[tp, b] = hid_ref[:, pl.ds(pl.multiple_of((quarter + 4 * b) * 512, 512), 512)]
+    pl.semaphore_wait(barrier, len(peers))
+
+    def spread(r, b):
+        device = at_tp(r)
+        if b == 2:
+            src, dst = scl.at[tp], scl.at[tp]
+        else:
+            block = lax.rem(device[0], 4) + 4 * b
+            src, dst = hid_ref.at[:, pl.ds(pl.multiple_of(block * 512, 512), 512)], hq.at[tp, b]
+        return move(src, dst, p_s.at[r - 1, b], p_r.at[r - 1, b], device)
+
+    for r in range(1, 8):
+        for b in range(3):
+            spread(r, b).start()
     loads = []
     for q in range(4):
         for b in range(2):
@@ -63,12 +86,6 @@
     loads.append(pltpu.make_async_copy(wd_ref.at[0], wdv, wsem.at[16]))
     for load in loads:
         load.start()
-
-    values = hid_ref[...].astype(F32)
-    scale = lax.rsqrt(jnp.mean(values * values, axis=1, keepdims=True) + 1e-06)
-    scl[tp] = jnp.broadcast_to(scale, (8, 128))
-    for b in range(2):
-        hq[tp, b] = hid_ref[:, pl.ds(pl.multiple_of((quarter + 4 * b) * 512, 512), 512)]
     ids, gates = ids_ref[...].astype(F32), gat_ref[...]
     meta = jnp.concatenate(
         [jnp.concatenate([ids, ids], axis=1), jnp.concatenate([gates, gates], axis=1)], axis=0
@@ -77,27 +94,13 @@
     meta_b[0] = meta
     before, after = lax.broadcasted_iota(jnp.int32, (128, 128), 0), lax.broadcasted_iota(jnp.int32, (128, 128), 1)
     tri[...] = ((before < after) & ((before < 64) == (after < 64))).astype(F32).astype(BF16)
-    pl.semaphore_wait(barrier, len(peers))
-
-    def spread(r, b):
-        device = at_tp(r)
-        if b == 2:
-            src, dst = scl.at[tp], scl.at[tp]
-        else:
-            block = lax.rem(device[0], 4) + 4 * b
-            src, dst = hid_ref.at[:, pl.ds(pl.multiple_of(block * 512, 512), 512)], hq.at[tp, b]
-        return move(src, dst, p_s.at[r - 1, b], p_r.at[r - 1, b], device)
-
-    for r in range(1, 8):
-        for b in range(3):
-            spread(r, b).start()
     for r in range(1, 8):
         for b in range(3):
             spread(r, b).wait_recv()
     scales = scl[...]
     scales = jnp.concatenate([scales] * 4, axis=2)
     for b in range(2):
-        gain = gain_ref[pl.ds(quarter + 4 * b, 1), :]
+        gain = gain_ref[pl.ds(pl.multiple_of((quarter + 4 * b) * 512, 512), 512)].astype(F32).reshape(1, 512)
         normed = (hq[:, b].astype(F32) * scales).reshape(64, 512) * gain
         normed = normed.astype(BF16)
         ring_a[0, b] = normed
@@ -106,17 +109,19 @@
         load.wait()
 
     def up(i, b):
-        if b == 2:
+        if b == PARTS:
             src, dst = meta_a.at[i], meta_a.at[i + 1]
         else:
-            src, dst = ring_a.at[i, b], ring_a.at[i + 1, b]
+            cols = pl.ds(b * 1024 // PARTS % 512, 1024 // PARTS)
+            src, dst = ring_a.at[i, b * 2 // PARTS, :, cols], ring_a.at[i + 1, b * 2 // PARTS, :, cols]
         return move(src, dst, za_s.at[i, b], za_r.at[i, b], at_z(1))
 
     def down(i, b):
-        if b == 2:
+        if b == PARTS:
             src, dst = meta_b.at[i], meta_b.at[i + 1]
         else:
-            src, dst = ring_b.at[i, b], ring_b.at[i + 1, b]
+            cols = pl.ds(b * 1024 // PARTS % 512, 1024 // PARTS)
+            src, dst = ring_b.at[i, b * 2 // PARTS, :, cols], ring_b.at[i + 1, b * 2 // PARTS, :, cols]
         return move(src, dst, zb_s.at[i, b], zb_r.at[i, b], at_z(-1))
 
     def to_y(j, r):
@@ -148,11 +153,11 @@
     def to_o(j, r):
         return move(obuf.at[j, lax.rem(y + r, 4)], oin.at[j, y], o_s.at[j, r - 1], o_r.at[j, r - 1], at_y(r))
 
-    def home_a(j, hops):
-        return move(cbuf.at[j, 0], zin_a.at[j], ra_s.at[j], ra_r.at[j], at_z(-hops))
-
-    def home_b(j, hops):
-        return move(cbuf.at[j, 1], zin_b.at[j], rb_s.at[j], rb_r.at[j], at_z(hops))
+    def home_a(j, d):
+        return move(cbuf.at[j, 0], zin_a.at[j], ra_s.at[j], ra_r.at[j], at_z(NEXT[d] - d))
+
+    def home_b(j, d):
+        return move(cbuf.at[j, 1], zin_b.at[j], rb_s.at[j], rb_r.at[j], at_z(d - NEXT[d]))
 
     def stage_y(j):
         first = lax.broadcasted_iota(jnp.int32, (8, 128), 1) < 64
@@ -238,33 +243,39 @@
         cbuf[j, 0] = total[:64].astype(BF16)
         cbuf[j, 1] = total[64:].astype(BF16)
 
-        @pl.when(j < 3)
-        def _():
-            home_a(j, j + 1).start()
-
-        @pl.when(j == 3)
-        def _():
-            own[0] = total[:64]
-
-        @pl.when(j > 3)
-        def _():
-            home_a(j, j - 3).start()
-
-        @pl.when(j == 0)
-        def _():
-            own[1] = total[64:]
-
-        @pl.when((j > 0) & (j < 4))
-        def _():
-            home_b(j, j).start()
-
-        @pl.when(j == 4)
-        def _():
-            own[2] = total[64:]
-
-        @pl.when(j > 4)
-        def _():
-            home_b(j, j - 4).start()
+        for d in range(9):
+            if d:
+                @pl.when(j + 1 == d)
+                def _():
+                    if d in HOLDS:
+                        own[1 + HOLDS.index(d), 0] = total[:64]
+                    else:
+                        home_a(d - 1, d).start()
+
+            if d < 8:
+                @pl.when(j == d)
+                def _():
+                    if d == 0:
+                        own[0, 0] = total[64:]
+                    elif d in HOLDS:
+                        own[1 + HOLDS.index(d), 1] = total[64:]
+                    else:
+                        home_b(d, d).start()
+
+        for b in range(PARTS + 1):
+            up(j, b).wait_send()
+
+            @pl.when(j < STEPS - 1)
+            def _():
+                down(j, b).wait_send()
+
+        for r in range(1, 4):
+            to_y(j, r).wait_send()
+            to_o(j, r).wait_send()
+        for n in range(4):
+            to_x(j, n).wait_send()
+        for n in range(7):
+            to_h(j, n).wait_send()
 
     def stage(name, body, i):
         j = i - AT[name]
@@ -277,7 +288,7 @@
     def _(i):
         @pl.when(i <= STEPS)
         def _():
-            for b in (2, 0, 1):
+            for b in range(PARTS + 1):
 
                 @pl.when(i > 0)
                 def _():
@@ -303,55 +314,35 @@
         stage("M", stage_m, i)
         stage("C", stage_c, i)
 
-    total = own[0]
-    for j in range(4, 8):
-        home_a(j, 0).wait_recv()
-        total += zin_a[j].astype(F32)
-    cbuf[3, 0] = total.astype(BF16)
-    home_a(3, 4).start()
-    total = own[2]
-    for j in range(5, 8):
-        home_b(j, 0).wait_recv()
-        total += zin_b[j].astype(F32)
-    cbuf[4, 1] = total.astype(BF16)
-    home_b(4, 4).start()
-
-    total = own[1] + hq[:, tp // 4].astype(F32).reshape(64, 512)
-    for j in range(3):
-        home_a(j, 0).wait_recv()
-        total += zin_a[j].astype(F32)
-    for j in range(1, 4):
-        home_b(j, 0).wait_recv()
-        total += zin_b[j].astype(F32)
-    home_a(3, 4).wait_recv()
-    home_b(4, 4).wait_recv()
-    out_ref[...] = (total + zin_a[3].astype(F32) + zin_b[4].astype(F32)).astype(BF16)
+    for d in HOLDS:
+        for n, home, zin in ((0, home_a, zin_a), (1, home_b, zin_b)):
+            total = own[1 + HOLDS.index(d), n]
+            for e in range(7 + (n == 0), d, -1):
+                if NEXT[e] == d:
+                    home(e - (n == 0), e).wait_recv()
+                    total += zin[e - (n == 0)].astype(F32)
+            cbuf[d - (n == 0), n] = total.astype(BF16)
+            home(d - (n == 0), d).start()
 
     for r in range(1, 8):
         for b in range(3):
             spread(r, b).wait_send()
-
-    @pl.loop(0, STEPS)
-    def _(j):
-        for b in range(3):
-            up(j, b).wait_send()
-
-            @pl.when(j < STEPS - 1)
-            def _():
-                down(j, b).wait_send()
-
-        for r in range(1, 4):
-            to_y(j, r).wait_send()
-            to_o(j, r).wait_send()
-        for n in range(4):
-            to_x(j, n).wait_send()
-        for n in range(7):
-            to_h(j, n).wait_send()
-        home_a(j, 1).wait_send()
-
-        @pl.when(j > 0)
-        def _():
-            home_b(j, 1).wait_send()
+    total = own[0, 0] + hq[:, tp // 4].astype(F32).reshape(64, 512)
+    for d in range(1, 9):
+        if NEXT[d] == 0 and d not in HOLDS:
+            home_a(d - 1, d).wait_recv()
+            home_b(d, d).wait_recv()
+            total += zin_a[d - 1].astype(F32) + zin_b[d].astype(F32)
+    for d in range(1, 9):
+        home_a(d - 1, d).wait_send()
+        if d < 8:
+            home_b(d, d).wait_send()
+    for d in reversed(HOLDS):
+        if NEXT[d] == 0:
+            home_a(d - 1, d).wait_recv()
+            home_b(d, d).wait_recv()
+            total += zin_a[d - 1].astype(F32) + zin_b[d].astype(F32)
+    out_ref[...] = total.astype(BF16)
 
 
 def shards(hidden_in, norm_gain, expert_ids, gate_weights, w_gate, w_up, w_down):
@@ -376,7 +367,7 @@
             pltpu.VMEM((8, 4, 32, 512), BF16),
             pltpu.VMEM((8, 4, 32, 512), BF16),
             pltpu.VMEM((8, 2, 64, 512), BF16),
-            pltpu.VMEM((3, 64, 512), F32),
+            pltpu.VMEM((1 + len(HOLDS), 2, 64, 512), F32),
             pltpu.VMEM((8, 64, 512), BF16),
             pltpu.VMEM((8, 64, 512), BF16),
             pltpu.VMEM((4, 1024, 256), BF16),
@@ -384,8 +375,8 @@
             pltpu.VMEM((128, 128), BF16),
             dma((17,)),
             dma((7, 3)), dma((7, 3)),
-            dma((8, 3)), dma((8, 3)),
-            dma((7, 3)), dma((7, 3)),
+            dma((8, PARTS + 1)), dma((8, PARTS + 1)),
+            dma((7, PARTS + 1)), dma((7, PARTS + 1)),
             dma((8, 3)), dma((8, 3)),
             dma((8, 4)), dma((8, 4)),
             dma((8, 7)), dma((8, 7)),
@@ -398,7 +389,7 @@
         ),
     )(
         hidden_in,
-        norm_gain.astype(F32).reshape(8, 512),
+        norm_gain,
         expert_ids.T,
         gate_weights.T,
         w_gate,

time: 109 us -> 102 us (0.936)
  the two profiles are of different devices: /device:TPU:1 before, /device:TPU:8 now
where the time goes in v2:
time: 102 us
  Pallas kernels  100 us (98%)
  local copies, waits for them, and re-layouts  1.47 us (1%)
    pallas_call x1, Pallas kernels, shards(): pl.pallas_call(kernel, out_shape=jax.ShapeDtypeStruct((64, 512), BF16), i...  100 us

profile of v2, /device:TPU:8, one launch (start us, length us, event | category | flops | bytes accessed | tf_op | source)
XLA Modules:
  0.0 102.0 jit_solution(1931044884749931975)
XLA Ops:
  0.0 100.5 %shard_map.73 = bf16[64,512]{1,0:T(8,128)(2,1)} custom-call(bf16[8,4096]{1,0:T(8,128)(2,1)} %hid_ref.1, bf16[4096]{0:T(1024)(128)(2,1)} %gain_ref.1, s32[8,64]{1,0:T(8,128)} %bitcast.2, f32[8,64]{1,0:T(8,128)} %bitcast.3, bf16[1,4096,128]{2,1,0:T(8,128)(2,1)} %wg_ref.1, bf16[1,4096,128]{2,1,0:T(8,128)(2,1)} %wu_ref.1, bf16[1,1024,512]{2,1,0:T(8,128)(2,1)} %wd_ref.1), custom_call_target="tpu_custom_call" | custom-call | tf_op jit(solution)/shard_map/pallas_call | solution.py:351
  100.5 1.5 %copy.9 = bf16[64,512]{1,0:T(8,128)(2,1)} copy(bf16[64,512]{1,0:T(8,128)(2,1)} %shard_map.73) | data formatting | bytes 131072

commit v3 on v2

v3 whole, which is shorter than its diff:
```python
import functools

import jax
import jax.numpy as jnp
from jax import lax
from jax.experimental import pallas as pl
from jax.experimental.pallas import tpu as pltpu
from jax.sharding import PartitionSpec as P

MESH = pl.DeviceIdType.MESH
F32, BF16 = jnp.float32, jnp.bfloat16
CHUNKS = 16
PARTS = 2
AT = {'Y': 0, 'X1': 2, 'X2': 4, 'M': 6, 'H2': 8, 'D': 9, 'C': 12}


def kernel(
    hid_ref, gain_ref, ids_ref, gat_ref, wg_ref, wu_ref, wd_ref, out_ref,
    hq, scl, ring, meta, pick, ybuf, xfull, hfull, obuf, oin, cbuf, own, zin,
    wcat, wdv, tri,
    wsem, p_s, p_r, z_s, z_r, y_s, y_r, x_s, x_r, h_s, h_r, o_s, o_r, c_s, c_r,
):
    tp, ep = lax.axis_index("tp"), lax.axis_index("ep")
    x, c = tp // 2, lax.rem(tp, 2)
    z, y = ep // 4, lax.rem(ep, 4)
    quarter = lax.rem(tp, 4)
    across = lax.rem(quarter + 2, 4)

    def at_tp(r):
        return (lax.rem(tp + r + 8, 8), ep)

    def at_x(r):
        return (lax.rem(x + r + 4, 4) * 2 + c, ep)

    def at_y(r):
        return (tp, z * 4 + lax.rem(y + r, 4))

    def at_z(r):
        return (tp, lax.rem(z + r + 16, 16) * 4 + y)

    partner = (x * 2 + 1 - c, ep)

    def move(src, dst, send, recv, device):
        return pltpu.make_async_remote_copy(
            src_ref=src, dst_ref=dst, send_sem=send, recv_sem=recv, device_id=device, device_id_type=MESH
        )

    barrier = pltpu.get_barrier_semaphore()
    peers = [at_tp(r) for r in range(1, 8)] + [at_y(r) for r in range(1, 4)]
    peers += [at_z(r) for r in (-3, -2, -1, 1, 2, 3)]
    for peer in peers:
        pl.semaphore_signal(barrier, inc=1, device_id=peer, device_id_type=MESH)

    values = hid_ref[...].astype(F32)
    scale = lax.rsqrt(jnp.mean(values * values, axis=1, keepdims=True) + 1e-06)
    scl[tp] = jnp.broadcast_to(scale, (8, 128))
    for b in range(2):
        hq[tp, b] = hid_ref[:, pl.ds(pl.multiple_of((quarter + 4 * b) * 512, 512), 512)]
    pl.semaphore_wait(barrier, len(peers))

    def spread(r, b):
        device = at_tp(r)
        if b == 2:
            src, dst = scl.at[tp], scl.at[tp]
        else:
            block = lax.rem(device[0], 4) + 4 * b
            src, dst = hid_ref.at[:, pl.ds(pl.multiple_of(block * 512, 512), 512)], hq.at[tp, b]
        return move(src, dst, p_s.at[r - 1, b], p_r.at[r - 1, b], device)

    for r in range(1, 8):
        for b in range(3):
            spread(r, b).start()
    loads = []
    for q in range(4):
        for b in range(2):
            rows = pl.ds((q + 4 * b) * 512, 512)
            for n, w in enumerate((wg_ref, wu_ref)):
                loads.append(
                    pltpu.make_async_copy(
                        w.at[0, rows, :], wcat.at[q, pl.ds(b * 512, 512), pl.ds(n * 128, 128)], wsem.at[len(loads)]
                    )
                )
    loads.append(pltpu.make_async_copy(wd_ref.at[0], wdv, wsem.at[16]))
    for load in loads:
        load.start()
    ids, gates = ids_ref[...].astype(F32), gat_ref[...]
    table = jnp.concatenate(
        [jnp.concatenate([ids, ids], axis=1), jnp.concatenate([gates, gates], axis=1)], axis=0
    )
    meta[0] = table
    meta[1] = table
    before, after = lax.broadcasted_iota(jnp.int32, (64, 64), 0), lax.broadcasted_iota(jnp.int32, (64, 64), 1)
    tri[...] = (before < after).astype(F32).astype(BF16)
    for r in range(1, 8):
        for b in range(3):
            spread(r, b).wait_recv()
    scales = scl[...]
    scales = jnp.concatenate([scales] * 4, axis=2)
    for b in range(2):
        gain = gain_ref[pl.ds(pl.multiple_of((quarter + 4 * b) * 512, 512), 512)].astype(F32).reshape(1, 512)
        normed = (hq[:, b].astype(F32) * scales).reshape(64, 512) * gain
        normed = normed.astype(BF16)
        ring[0, b] = normed
        ring[1, b] = normed
    for load in loads:
        load.wait()

    def pass_on(r, b):
        if b == PARTS:
            src, dst = meta.at[r], meta.at[r + 2]
        else:
            cols = pl.ds(b * 1024 // PARTS % 512, 1024 // PARTS)
            src, dst = ring.at[r, b * 2 // PARTS, :, cols], ring.at[r + 2, b * 2 // PARTS, :, cols]
        return move(src, dst, z_s.at[r, b], z_r.at[r, b], at_z(1 - 2 * lax.rem(r, 2)))

    def to_y(j, r):
        device = at_y(r)
        there = lax.rem(y + r, 4)
        dst = xfull.at[j, quarter, pl.ds(pl.multiple_of(y * 16, 16), 16), :]
        return move(ybuf.at[j, there], dst, y_s.at[j, r - 1], y_r.at[j, r - 1], device)

    def to_x(j, n):
        if n == 0:
            part, device = xfull.at[j, quarter, pl.ds(0, 32), :], at_x(1)
        elif n == 1:
            part, device = xfull.at[j, quarter, pl.ds(32, 32), :], at_x(-1)
        elif n == 2:
            part, device = xfull.at[j, quarter], partner
        else:
            part, device = xfull.at[j, across], partner
        return move(part, part, x_s.at[j, n], x_r.at[j, n], device)

    def to_h(j, n):
        if n < 3:
            part, device = hfull.at[j, tp], at_x(n + 1)
        elif n == 3:
            part, device = hfull.at[j, tp], partner
        else:
            part, device = hfull.at[j, lax.rem(tp - 2 * (n - 3) + 8, 8)], partner
        return move(part, part, h_s.at[j, n], h_r.at[j, n], device)

    def to_o(j, r):
        return move(obuf.at[j, lax.rem(y + r, 4)], oin.at[j, y], o_s.at[j, r - 1], o_r.at[j, r - 1], at_y(r))

    def home(j, hops):
        away = (2 * lax.rem(j + 1, 2) - 1) * hops
        return move(cbuf.at[j], zin.at[j], c_s.at[j], c_r.at[j], at_z(away))

    def stage_y(j):
        ids, gates = meta[j + 1, 0:8, 0:64], meta[j + 1, 8:16, 0:64]
        row = lax.broadcasted_iota(jnp.int32, (16, 64), 0)
        hits, weights, table = [], [], jnp.zeros((16, 64), F32)
        for n in range(4):
            same = ids == (z * 4 + n).astype(F32)
            hits.append(jnp.sum(jnp.where(same, 1.0, 0.0), axis=0, keepdims=True))
            weights.append(jnp.sum(jnp.where(same, gates, 0.0), axis=0, keepdims=True))
            table = jnp.where(row == n, hits[n], table)
        places = jnp.dot(table.astype(BF16), tri[...], preferred_element_type=F32)
        slot = row.astype(F32)
        chosen, weighted = [], []
        for n in range(4):
            mine = jnp.where(hits[n] > 0.5, places[n : n + 1], -1.0)
            chosen.append(jnp.where(slot == mine, 1.0, 0.0))
            weighted.append(chosen[n] * weights[n])
        chosen = jnp.concatenate(chosen, axis=0).astype(BF16)
        weighted = jnp.concatenate(weighted, axis=0)
        high = weighted.astype(BF16)
        pick[j, 0] = high
        pick[j, 1] = (weighted - high.astype(F32)).astype(BF16)
        for b in range(2):
            rows = jnp.dot(chosen, ring[j + 1, b], preferred_element_type=F32).astype(BF16)
            ybuf[j, :, :, pl.ds(b * 512, 512)] = rows.reshape(4, 16, 512)
        xfull[j, quarter, pl.ds(pl.multiple_of(y * 16, 16), 16), :] = ybuf[j, y]
        for r in range(1, 4):
            to_y(j, r).start()

    def stage_x1(j):
        for r in range(1, 4):
            to_y(j, r).wait_recv()
        for n in range(3):
            to_x(j, n).start()

    def stage_x2(j):
        for n in range(2):
            wait_x(j, n)
        to_x(j, 3).start()

    def wait_x(j, n):
        part = xfull.at[j, across, pl.ds(32 * n, 32), :]
        move(part, part, x_s.at[j, n], x_r.at[j, n], partner).wait_recv()

    def stage_m(j):
        for n in range(2, 4):
            to_x(j, n).wait_recv()
        total = jnp.zeros((64, 256), F32)
        for q in range(4):
            total += jnp.dot(xfull[j, q], wcat[q], preferred_element_type=F32)
        gate, lift = total[:, :128], total[:, 128:]
        hfull[j, tp] = (gate / (1.0 + jnp.exp(-gate)) * lift).astype(BF16)
        for n in range(4):
            to_h(j, n).start()

    def stage_h2(j):
        for n in range(3):
            to_h(j, n).wait_recv()
        for n in range(4, 7):
            to_h(j, n).start()

    def stage_d(j):
        for n in range(3, 7):
            to_h(j, n).wait_recv()
        units = jnp.concatenate([hfull[j, n] for n in range(8)], axis=1)
        rows = jnp.dot(units, wdv[...], preferred_element_type=F32).astype(BF16)
        obuf[j] = rows.reshape(4, 16, 512)
        oin[j, y] = obuf[j, y]
        for r in range(1, 4):
            to_o(j, r).start()

    def stage_c(j):
        for r in range(1, 4):
            to_o(j, r).wait_recv()
        rows = oin[j].reshape(64, 512)
        dims = (((0,), (0,)), ((), ()))
        total = lax.dot_general(pick[j, 0], rows, dims, preferred_element_type=F32)
        total += lax.dot_general(pick[j, 1], rows, dims, preferred_element_type=F32)
        cbuf[j] = total.astype(BF16)
        distance = (j + 1) // 2

        @pl.when(lax.rem(distance, 3) > 0)
        def _():
            home(j, lax.rem(distance, 3)).start()

        @pl.when(lax.rem(distance, 3) == 0)
        def _():
            own[distance // 3, lax.rem(j, 2)] = total

        @pl.when(j < 15)
        def _():
            for b in range(PARTS + 1):
                pass_on(j, b).wait_send()

        for r in range(1, 4):
            to_y(j, r).wait_send()
            to_o(j, r).wait_send()
        for n in range(4):
            to_x(j, n).wait_send()
        for n in range(7):
            to_h(j, n).wait_send()

    def stage(name, body, i):
        j = i - AT[name]

        @pl.when((j >= 0) & (j < CHUNKS))
        def _():
            body(j)

    for r in range(2):
        for b in range(PARTS + 1):
            pass_on(r, b).start()

    @pl.loop(0, CHUNKS + AT["C"])
    def _(i):
        @pl.when((i > 0) & (i < CHUNKS))
        def _():
            for b in range(PARTS + 1):
                pass_on(i - 1, b).wait_recv()

                @pl.when(i < 14)
                def _():
                    pass_on(i + 1, b).start()

        stage("Y", stage_y, i)
        stage("C", stage_c, i)
        stage("X1", stage_x1, i)
        stage("M", stage_m, i)
        stage("D", stage_d, i)
        stage("X2", stage_x2, i)
        stage("H2", stage_h2, i)

    for d in (6, 3):
        for j in (2 * d - 1, 2 * d):
            total = own[d // 3, j % 2]
            for e in range(j + 6 if d == 3 else j + 4, j, -2):
                if e < CHUNKS:
                    home(e, 0).wait_recv()
                    total += zin[e].astype(F32)
            cbuf[j] = total.astype(BF16)
            home(j, 3).start()

    for r in range(1, 8):
        for b in range(3):
            spread(r, b).wait_send()
    total = own[0, 0] + hq[:, tp // 4].astype(F32).reshape(64, 512)
    for j in range(1, 5):
        home(j, 0).wait_recv()
        total += zin[j].astype(F32)
    for j in range(1, CHUNKS):
        home(j, 0).wait_send()
    for j in range(5, 7):
        home(j, 0).wait_recv()
        total += zin[j].astype(F32)
    out_ref[...] = total.astype(BF16)


def shards(hidden_in, norm_gain, expert_ids, gate_weights, w_gate, w_up, w_down):
    vmem, hbm = pl.BlockSpec(memory_space=pltpu.VMEM), pl.BlockSpec(memory_space=pl.ANY)
    dma = pltpu.SemaphoreType.DMA
    return pl.pallas_call(
        kernel,
        out_shape=jax.ShapeDtypeStruct((64, 512), BF16),
        in_specs=[vmem] * 4 + [hbm] * 3,
        out_specs=vmem,
        scratch_shapes=[
            pltpu.VMEM((8, 2, 8, 512), BF16),
            pltpu.VMEM((8, 8, 128), F32),
            pltpu.VMEM((17, 2, 64, 512), BF16),
            pltpu.VMEM((17, 16, 128), F32),
            pltpu.VMEM((16, 2, 64, 64), BF16),
            pltpu.VMEM((16, 4, 16, 1024), BF16),
            pltpu.VMEM((16, 4, 64, 1024), BF16),
            pltpu.VMEM((16, 8, 64, 128), BF16),
            pltpu.VMEM((16, 4, 16, 512), BF16),
            pltpu.VMEM((16, 4, 16, 512), BF16),
            pltpu.VMEM((16, 64, 512), BF16),
            pltpu.VMEM((3, 2, 64, 512), F32),
            pltpu.VMEM((16, 64, 512), BF16),
            pltpu.VMEM((4, 1024, 256), BF16),
            pltpu.VMEM((1024, 512), BF16),
            pltpu.VMEM((64, 64), BF16),
            dma((17,)),
            dma((7, 3)), dma((7, 3)),
            dma((15, PARTS + 1)), dma((15, PARTS + 1)),
            dma((16, 3)), dma((16, 3)),
            dma((16, 4)), dma((16, 4)),
            dma((16, 7)), dma((16, 7)),
            dma((16, 3)), dma((16, 3)),
            dma((16,)), dma((16,)),
        ],
        compiler_params=pltpu.CompilerParams(
            collective_id=0, has_side_effects=True, vmem_limit_bytes=56 * 1024 * 1024
        ),
    )(
        hidden_in,
        norm_gain,
        expert_ids.T,
        gate_weights.T,
        w_gate,
        w_up,
        w_down,
    )


def solution(mesh):
    in_specs = (
        P(("ep", "tp"), None),
        P(),
        P("ep", None),
        P("ep", None),
        P("ep", None, "tp"),
        P("ep", None, "tp"),
        P("ep", None, "tp"),
    )
    return jax.shard_map(shards, mesh=mesh, in_specs=in_specs, out_specs=P("ep", "tp"), check_vma=False)
```

time: 102 us -> 99.7 us (0.977)
  Pallas kernels: 100 us -> 97.4 us
    pallas_call x1, Pallas kernels: 100 us -> 97.4 us  [shards(): pl.pallas_call(kernel, out_shape=jax.ShapeDtypeStruct((64, 512), BF16), i...]
where the time goes in v3:
time: 99.7 us; the launch traced here: 98.9 us
  Pallas kernels  97.4 us (98%)
  local copies, waits for them, and re-layouts  1.47 us (1%)
    pallas_call x1, Pallas kernels, shards(): pl.pallas_call(kernel, out_shape=jax.ShapeDtypeStruct((64, 512), BF16), i...  97.4 us

profile of v3, /device:TPU:8, one launch (start us, length us, event | category | flops | bytes accessed | tf_op | source)
XLA Modules:
  0.0 98.9 jit_solution(6222624591987734336)
XLA Ops:
  0.0 97.4 %shard_map.73 = bf16[64,512]{1,0:T(8,128)(2,1)} custom-call(bf16[8,4096]{1,0:T(8,128)(2,1)} %hid_ref.1, bf16[4096]{0:T(1024)(128)(2,1)} %gain_ref.1, s32[8,64]{1,0:T(8,128)} %bitcast.2, f32[8,64]{1,0:T(8,128)} %bitcast.3, bf16[1,4096,128]{2,1,0:T(8,128)(2,1)} %wg_ref.1, bf16[1,4096,128]{2,1,0:T(8,128)(2,1)} %wu_ref.1, bf16[1,1024,512]{2,1,0:T(8,128)(2,1)} %wd_ref.1), custom_call_target="tpu_custom_call" | custom-call | tf_op jit(solution)/shard_map/pallas_call | solution.py:308
  97.4 1.5 %copy.9 = bf16[64,512]{1,0:T(8,128)(2,1)} copy(bf16[64,512]{1,0:T(8,128)(2,1)} %shard_map.73) | data formatting | bytes 131072

commit v4 on v3

--- a/solution.py
+++ b/solution.py
@@ -15,10 +15,11 @@
 
 
 def kernel(
-    hid_ref, gain_ref, ids_ref, gat_ref, wg_ref, wu_ref, wd_ref, out_ref,
+    hid_in, gain_in, ids_in, gat_in, wg_ref, wu_ref, wd_ref, out_ref,
+    hid_ref, gain_ref, ids_ref, gat_ref,
     hq, scl, ring, meta, pick, ybuf, xfull, hfull, obuf, oin, cbuf, own, zin,
     wcat, wdv, tri,
-    wsem, p_s, p_r, z_s, z_r, y_s, y_r, x_s, x_r, h_s, h_r, o_s, o_r, c_s, c_r,
+    isem, wsem, p_s, p_r, z_s, z_r, y_s, y_r, x_s, x_r, h_s, h_r, o_s, o_r, c_s, c_r,
 ):
     tp, ep = lax.axis_index("tp"), lax.axis_index("ep")
     x, c = tp // 2, lax.rem(tp, 2)
@@ -51,6 +52,16 @@
     for peer in peers:
         pl.semaphore_signal(barrier, inc=1, device_id=peer, device_id_type=MESH)
 
+    takes = [
+        pltpu.make_async_copy(src, dst, isem.at[n])
+        for n, (src, dst) in enumerate(
+            ((hid_in, hid_ref), (gain_in, gain_ref), (ids_in, ids_ref), (gat_in, gat_ref))
+        )
+    ]
+    for take in takes:
+        take.start()
+    for take in takes:
+        take.wait()
     values = hid_ref[...].astype(F32)
     scale = lax.rsqrt(jnp.mean(values * values, axis=1, keepdims=True) + 1e-06)
     scl[tp] = jnp.broadcast_to(scale, (8, 128))
@@ -308,9 +319,13 @@
     return pl.pallas_call(
         kernel,
         out_shape=jax.ShapeDtypeStruct((64, 512), BF16),
-        in_specs=[vmem] * 4 + [hbm] * 3,
+        in_specs=[hbm] * 7,
         out_specs=vmem,
         scratch_shapes=[
+            pltpu.VMEM((8, 4096), BF16),
+            pltpu.VMEM((4096,), BF16),
+            pltpu.VMEM((8, 64), jnp.int32),
+            pltpu.VMEM((8, 64), F32),
             pltpu.VMEM((8, 2, 8, 512), BF16),
             pltpu.VMEM((8, 8, 128), F32),
             pltpu.VMEM((17, 2, 64, 512), BF16),
@@ -327,6 +342,7 @@
             pltpu.VMEM((4, 1024, 256), BF16),
             pltpu.VMEM((1024, 512), BF16),
             pltpu.VMEM((64, 64), BF16),
+            dma((4,)),
             dma((17,)),
             dma((7, 3)), dma((7, 3)),
             dma((15, PARTS + 1)), dma((15, PARTS + 1)),

time: 99.7 us -> 99 us (level)
  no operation moved by 1% of the time
where the time goes in v4:
time: 99 us; the launch traced here: 98.8 us
  Pallas kernels  97.3 us (98%)
  local copies, waits for them, and re-layouts  1.47 us (1%)
    pallas_call x1, Pallas kernels, shards(): pl.pallas_call(kernel, out_shape=jax.ShapeDtypeStruct((64, 512), BF16), i...  97.3 us

profile of v4, /device:TPU:8, one launch (start us, length us, event | category | flops | bytes accessed | tf_op | source)
XLA Modules:
  0.0 98.8 jit_solution(18268990578690815884)
XLA Ops:
  0.0 97.3 %shard_map.73 = bf16[64,512]{1,0:T(8,128)(2,1)} custom-call(bf16[8,4096]{1,0:T(8,128)(2,1)} %hid_in.1, bf16[4096]{0:T(1024)(128)(2,1)} %gain_in.1, s32[8,64]{1,0:T(8,128)} %bitcast.2, f32[8,64]{1,0:T(8,128)} %bitcast.3, bf16[1,4096,128]{2,1,0:T(8,128)(2,1)} %wg_ref.1, bf16[1,4096,128]{2,1,0:T(8,128)(2,1)} %wu_ref.1, bf16[1,1024,512]{2,1,0:T(8,128)(2,1)} %wd_ref.1), custom_call_target="tpu_custom_call" | custom-call | tf_op jit(solution)/shard_map/pallas_call | solution.py:319
  97.3 1.5 %copy.9 = bf16[64,512]{1,0:T(8,128)(2,1)} copy(bf16[64,512]{1,0:T(8,128)(2,1)} %shard_map.73) | data formatting | bytes 131072
